TPU v7x, 256 devices: a whole 4x4x8 slice. The times are simulated.
256 devices in a mesh: dp: 16 (over x, y), expert: 16 (over z, core).
Axes of the slice: x: 4, y: 4, z: 8, core: 2. Of those that a mesh axis runs over, the one named last changes fastest.
Arguments:
- tokens: bfloat16 [262144, 2048], P(('dp', 'expert')), may hold values from -16 to 16
- slot_param: bfloat16 [2048, 128], replicated, may hold values from -10 to 10
- pattern: int32 [128, 2048], P(None, ('dp', 'expert')), may hold values from 0 to 1, as said below
- w_in: bfloat16 [32, 2048, 4096], P('expert', None, 'dp'), may hold values from -0.125 to 0.125
- w_out: bfloat16 [32, 4096, 2048], P('expert', 'dp'), may hold values from -0.09375 to 0.09375
Outputs:
- mixed: bfloat16 [262144, 2048], P(('dp', 'expert'))
Inputs may be any that keep to these rules, and one draw needn't show every extreme that they name: `pattern`: every slot sees at least one block; about a quarter of all pairs are 1.
All inputs are finite; a program needn't handle non-finite values.
Results may differ from a plain program's by a relative error of at most 0.0095.
Values may be sent and summed in bfloat16 or wider, within the bound.
No kernel may reach another device: no remote copies, remote signals or barrier semaphores. Data moves between devices by JAX's collectives and lax.ppermute only.
A program may use at most 64 MiB of HBM per device.

v0:
```python
import jax
import jax.numpy as jnp
from jax import lax
from jax.sharding import PartitionSpec as P

D = 2048
EXP_DEV = 2
SLOTS = 4
BLOCK = 128
floor_value = -1e30


def local(tokens, slot_param, pattern, w_in, w_out):
    logits = jnp.dot(tokens, slot_param, preferred_element_type=jnp.float32)
    visible = jnp.repeat(pattern.T > 0, BLOCK, axis=0)
    local_peak = jnp.max(jnp.where(visible, logits, floor_value), axis=0)
    slot_peak = lax.pmax(local_peak, ("dp", "expert"))
    weights = jnp.where(visible, jnp.exp(logits - slot_peak[None, :]), 0.0).astype(jnp.bfloat16)
    weight_sum = jnp.sum(weights.astype(jnp.float32), axis=0)
    numerator = lax.dot_general(
        weights, tokens, (((0,), (0,)), ((), ())), preferred_element_type=jnp.float32
    )
    owned_num, owned_den = (
        lax.psum_scatter(numerator, "expert", scatter_dimension=0, tiled=True),
        lax.psum_scatter(weight_sum, "expert", scatter_dimension=0, tiled=True),
    )
    slot_num, slot_den = lax.psum((owned_num, owned_den), "dp")
    slot_in = (slot_num / slot_den[:, None]).astype(jnp.bfloat16)
    grouped = slot_in.reshape(EXP_DEV, SLOTS, D)
    hidden = jax.nn.gelu(
        jnp.einsum("esd,edh->esh", grouped, w_in, preferred_element_type=jnp.float32)
    ).astype(jnp.bfloat16)
    partial_value = jnp.einsum(
        "esh,ehd->esd", hidden, w_out, preferred_element_type=jnp.float32
    ).reshape(EXP_DEV * SLOTS, D)
    mixing = jax.nn.softmax(logits, axis=1).astype(jnp.bfloat16)
    owned_out = lax.psum(partial_value, "dp").astype(jnp.bfloat16)
    slot_out = lax.all_gather(owned_out, "expert", axis=0, tiled=True)
    result = jnp.dot(mixing, slot_out, preferred_element_type=jnp.float32)
    return result.astype(jnp.bfloat16)


def solution(mesh):
    return jax.shard_map(
        local,
        mesh=mesh,
        in_specs=(
            P(("dp", "expert"), None),
            P(),
            P(None, ("dp", "expert")),
            P("expert", None, "dp"),
            P("expert", "dp", None),
        ),
        out_specs=P(("dp", "expert"), None),
        check_vma=False,
    )
```

profile of v0, /device:TPU:1, one launch (start us, length us, event | category | flops | bytes accessed | tf_op | source)
XLA Modules:
  0.0 349.2 jit_solution(14017881914688491348)
XLA Ops:
  6.5 0.0 copy-start
  6.5 0.8 compare_bitcast_fusion
  7.4 3.6 %fusion.24 = (f32[1024]{0:T(1024)S(1)}, f32[1024,128]{1,0:T(8,128)S(1)}) fusion(bf16[1024,2048]{1,0:T(8,128)(2,1)} %param.5, bf16[2048,128]{1,0:T(8,128)(2,1)} %param.6), kind=kOutput, calls=%fused_computation.31 | convolution fusion | flops 537000960 | bytes 5246976 | tf_op jit(solution)/shard_map/dot_general | solution.py:14
  11.0 0.0 copy-start.1
  11.0 0.4 fusion.2
  11.4 81.4 %pmax.7 = f32[128]{0:T(128)S(1)} all-reduce(f32[128]{0:T(128)S(1)} %get-tuple-element.6), channel_id=1, replica_groups=mesh['dp'=16,'expert'=16] {'dp','expert'}, use_global_device_ids=true, to_apply=%region_3.4 | all-reduce | flops 128 | bytes 1024 | tf_op jit(solution)/shard_map/pmax | solution.py:17
  92.8 0.2 convert_reduce_fusion
  92.9 3.9 %fusion.27 = f32[128,2048]{1,0:T(8,128)} fusion(bf16[1024,128]{1,0:T(8,128)(2,1)S(1)} %get-tuple-element.8, bf16[1024,2048]{1,0:T(8,128)(2,1)} %param.5), kind=kOutput, calls=%fused_computation.33 | convolution fusion | flops 536870912 | bytes 5505024 | tf_op jit(solution)/shard_map/dot_general | solution.py:20
  96.8 0.0 reduce-scatter.2.cloned.1.call-update
  96.9 0.0 all-reduce.3.cloned.1.call-start
  96.9 50.6 %reduce-scatter.2.cloned.1.call-done = f32[8,2048]{1,0:T(8,128)} async-done(((f32[128,2048]{1,0:T(8,128)}), f32[8,2048]{1,0:T(8,128)}) %reduce-scatter.2.cloned.1.call-update) | async-done | bytes 65552 | tf_op jit(solution)/shard_map/reduce_scatter | solution.py:24
  147.5 0.0 all-reduce.3.cloned.1.call-update
  147.5 0.0 copy-done.1
  147.6 0.6 dynamic-slice
  148.8 26.4 %all-reduce = f32[128]{0:T(128)S(1)} all-reduce(f32[128]{0:T(128)S(1)} %get-tuple-element.7), channel_id=3, replica_groups=mesh['dp'=16,'expert'=16] {'expert'}, use_global_device_ids=true, to_apply=%region_7.8.clone | all-reduce | flops 128 | bytes 1024
  175.2 0.1 dynamic-slice.1
  175.2 33.7 %psum.22 = f32[8]{0:T(128)S(1)} all-reduce(f32[8]{0:T(128)S(1)} %dynamic-slice.1), channel_id=1, replica_groups=mesh['dp'=16,'expert'=16] {'dp'}, use_global_device_ids=true, to_apply=%region_8.9 | all-reduce | flops 8 | bytes 64 | tf_op jit(solution)/shard_map/psum | solution.py:27
  208.9 33.4 %all-reduce.3.cloned.1.call-done = f32[8,2048]{1,0:T(8,128)} async-done(((f32[8,2048]{1,0:T(8,128)}), f32[8,2048]{1,0:T(8,128)}) %all-reduce.3.cloned.1.call-update) | async-done | bytes 65552 | tf_op jit(solution)/shard_map/psum | solution.py:27
  242.4 0.9 divide_convert_fusion.2
  243.3 0.0 copy-done
  243.3 2.3 fusion.13
  245.7 58.1 %psum.23 = bf16[8,2048]{1,0:T(8,128)(2,1)S(1)} all-reduce(f32[8,2048]{1,0:T(8,128)S(1)} %reshape.15), channel_id=1, replica_groups=mesh['dp'=16,'expert'=16] {'dp'}, use_global_device_ids=true, to_apply=%region_9.10 | all-reduce | flops 16384 | bytes 98304 | tf_op jit(solution)/shard_map/psum | solution.py:37
  303.8 35.2 %all_gather.3 = bf16[128,2048]{1,0:T(8,128)(2,1)S(1)} all-gather(bf16[8,2048]{1,0:T(8,128)(2,1)S(1)} %psum.23), channel_id=1, replica_groups=mesh['dp'=16,'expert'=16] {'expert'}, dimensions={0}, use_global_device_ids=true | all-gather | bytes 557056 | tf_op jit(solution)/shard_map/all_gather | solution.py:38
  339.0 3.4 convolution_convert_fusion
  (3 shorter events, 0.1 us)
Async XLA Ops:
  6.5 236.8 %copy-start = (bf16[2,256,2048]{2,1,0:T(8,128)(2,1)S(1)}, bf16[2,256,2048]{2,1,0:T(8,128)(2,1)}, u32[]{:S(2)}) copy-start(bf16[2,256,2048]{2,1,0:T(8,128)(2,1)} %param.9) | copy-start | bytes 6291460
  6.5 141.0 %reduce-scatter.2.cloned.1.call-start = ((), (), s32[]{:S(2)}) async-start(), calls=%async_computation.1 | async-start | bytes 1114112 | tf_op jit(solution)/shard_map/reduce_scatter | solution.py:24
  11.0 136.5 %copy-start.1 = (u32[256]{0:T(256)S(1)}, u32[256]{0:T(256)}, u32[]{:S(2)}) copy-start(u32[256]{0:T(256)} %constant.22) | copy-start | bytes 3076
  96.9 145.5 %all-reduce.3.cloned.1.call-start = ((), (), s32[]{:S(2)}) async-start(), calls=%async_computation.2 | async-start | bytes 131072 | tf_op jit(solution)/shard_map/psum | solution.py:27
Sparse Core Ops, SparseCore 0:
  97.0 50.4 reduce-scatter.1
  150.7 91.6 all-reduce.2
where the time goes:
time: 350 us; the launch traced here: 349 us
  blocking collectives  235 us (67%)
  waiting for transfers between devices  84.1 us (24%)
  between operations  14.1 us (4%)
  matrix products  13.2 us (4%)
    pmax x1, blocking collectives, local(): slot_peak = lax.pmax(local_peak, ('dp', 'expert'))  81.4 us
    psum x1, blocking collectives, local(): owned_out = lax.psum(partial_value, 'dp').astype(jnp.bfloat16)  58.1 us
    reduce_scatter x1, waiting for transfers between devices, local(): lax.psum_scatter(numerator, 'expert', scatter_dimension=0, tiled=True)  50.6 us
    all_gather x1, blocking collectives, local(): slot_out = lax.all_gather(owned_out, 'expert', axis=0, tiled=True)  35.2 us
    psum x1, blocking collectives, local(): slot_num, slot_den = lax.psum((owned_num, owned_den), 'dp')  33.7 us
    psum x1, waiting for transfers between devices, local(): slot_num, slot_den = lax.psum((owned_num, owned_den), 'dp')  33.4 us
    unnamed x1, blocking collectives  26.4 us
  transfers between devices with their start and end apart: 2, of which 2 were waited for; matrix products, arithmetic and copies ran while one was open for 0% of the time, Pallas kernels for 0%

commit v1 on v0

--- a/solution.py
+++ b/solution.py
@@ -2,6 +2,7 @@
 import jax.numpy as jnp
 from jax import lax
 from jax.sharding import PartitionSpec as P
+from jax.lax import all_gather
 
 D = 2048
 EXP_DEV = 2
@@ -34,7 +35,8 @@
         "esh,ehd->esd", hidden, w_out, preferred_element_type=jnp.float32
     ).reshape(EXP_DEV * SLOTS, D)
     mixing = jax.nn.softmax(logits, axis=1).astype(jnp.bfloat16)
-    owned_out = lax.psum(partial_value, "dp").astype(jnp.bfloat16)
+    shape_stops_all = lambda slab_in: jnp.sum(all_gather(slab_in, "dp"), axis=0)
+    owned_out = shape_stops_all(partial_value).astype(jnp.bfloat16)
     slot_out = lax.all_gather(owned_out, "expert", axis=0, tiled=True)
     result = jnp.dot(mixing, slot_out, preferred_element_type=jnp.float32)
     return result.astype(jnp.bfloat16)

time: 350 us -> 326 us (0.931)
  blocking collectives: 235 us -> 163 us
  waiting for transfers between devices: 84.1 us -> 131 us
    psum x1 -> x0, blocking collectives: 58.1 us -> none  [local(): owned_out = lax.psum(partial_value, 'dp').astype(jnp.bfloat16)]
    all_gather x0 -> x1, waiting for transfers between devices: none -> 47.1 us  [local(): shape_stops_all = lambda slab_in: jnp.sum(all_gather(slab_in, 'dp'), axis=0)]
    all_gather x1, blocking collectives: 35.2 us -> 21.1 us  [local(): slot_out = lax.all_gather(owned_out, 'expert', axis=0, tiled=True)]
  transfers between devices with their start and end apart: 2 -> 3, of which waited for: 2 -> 3; matrix products, arithmetic and copies ran while one was open for 0% -> 0% of each run, Pallas kernels for 0% -> 0%
where the time goes in v1:
time: 326 us
  blocking collectives  163 us (50%)
  waiting for transfers between devices  131 us (40%)
  between operations  13.8 us (4%)
  matrix products  13.2 us (4%)
  other arithmetic  3.56 us (1%)
    pmax x1, blocking collectives, local(): slot_peak = lax.pmax(local_peak, ('dp', 'expert'))  81.4 us
    reduce_scatter x1, waiting for transfers between devices, local(): lax.psum_scatter(numerator, 'expert', scatter_dimension=0, tiled=True)  50.6 us
    all_gather x1, waiting for transfers between devices, local(): shape_stops_all = lambda slab_in: jnp.sum(all_gather(slab_in, 'dp'), axis=0)  47.1 us
    psum x1, blocking collectives, local(): slot_num, slot_den = lax.psum((owned_num, owned_den), 'dp')  33.6 us
    psum x1, waiting for transfers between devices, local(): slot_num, slot_den = lax.psum((owned_num, owned_den), 'dp')  33.4 us
    unnamed x1, blocking collectives  26.4 us
    all_gather x1, blocking collectives, local(): slot_out = lax.all_gather(owned_out, 'expert', axis=0, tiled=True)  21.1 us
  transfers between devices with their start and end apart: 3, of which 3 were waited for; matrix products, arithmetic and copies ran while one was open for 0% of the time, Pallas kernels for 0%

profile of v1, /device:TPU:1, one launch (start us, length us, event | category | flops | bytes accessed | tf_op | source)
XLA Modules:
  0.0 325.7 jit_solution(17764910509276290061)
XLA Ops:
  6.5 0.8 compare_bitcast_fusion
  7.4 3.6 %fusion.24 = (f32[1024]{0:T(1024)S(1)}, f32[1024,128]{1,0:T(8,128)S(1)}) fusion(bf16[1024,2048]{1,0:T(8,128)(2,1)} %param.5, bf16[2048,128]{1,0:T(8,128)(2,1)} %param.6), kind=kOutput, calls=%fused_computation.31 | convolution fusion | flops 537000960 | bytes 5246976 | tf_op jit(solution)/shard_map/dot_general | solution.py:15
  11.0 0.4 fusion.2
  11.4 81.4 %pmax.7 = f32[128]{0:T(128)S(1)} all-reduce(f32[128]{0:T(128)S(1)} %get-tuple-element.6), channel_id=1, replica_groups=mesh['dp'=16,'expert'=16] {'dp','expert'}, use_global_device_ids=true, to_apply=%region_3.4 | all-reduce | flops 128 | bytes 1024 | tf_op jit(solution)/shard_map/pmax | solution.py:18
  92.8 0.2 convert_reduce_fusion
  92.9 3.9 %fusion.27 = f32[128,2048]{1,0:T(8,128)} fusion(bf16[1024,128]{1,0:T(8,128)(2,1)S(1)} %get-tuple-element.8, bf16[1024,2048]{1,0:T(8,128)(2,1)} %param.5), kind=kOutput, calls=%fused_computation.33 | convolution fusion | flops 536870912 | bytes 5505024 | tf_op jit(solution)/shard_map/dot_general | solution.py:21
  96.8 0.0 reduce-scatter.2.cloned.1.call-update
  96.9 0.0 all-reduce.3.cloned.1.call-start
  96.9 50.6 %reduce-scatter.2.cloned.1.call-done = f32[8,2048]{1,0:T(8,128)} async-done(((f32[128,2048]{1,0:T(8,128)}), f32[8,2048]{1,0:T(8,128)}) %reduce-scatter.2.cloned.1.call-update) | async-done | bytes 65552 | tf_op jit(solution)/shard_map/reduce_scatter | solution.py:25
  147.5 0.0 all-reduce.3.cloned.1.call-update
  147.5 0.0 all-gather.2.cloned.1.call-start
  147.6 0.6 dynamic-slice
  148.8 26.4 %all-reduce = f32[128]{0:T(128)S(1)} all-reduce(f32[128]{0:T(128)S(1)} %get-tuple-element.7), channel_id=3, replica_groups=mesh['dp'=16,'expert'=16] {'expert'}, use_global_device_ids=true, to_apply=%region_7.8.clone | all-reduce | flops 128 | bytes 1024
  175.2 0.1 dynamic-slice.1
  175.3 33.6 %psum.15 = f32[8]{0:T(128)S(1)} all-reduce(f32[8]{0:T(128)S(1)} %dynamic-slice.1), channel_id=1, replica_groups=mesh['dp'=16,'expert'=16] {'dp'}, use_global_device_ids=true, to_apply=%region_8.9 | all-reduce | flops 8 | bytes 64 | tf_op jit(solution)/shard_map/psum | solution.py:28
  208.9 33.4 %all-reduce.3.cloned.1.call-done = f32[8,2048]{1,0:T(8,128)} async-done(((f32[8,2048]{1,0:T(8,128)}), f32[8,2048]{1,0:T(8,128)}) %all-reduce.3.cloned.1.call-update) | async-done | bytes 65552 | tf_op jit(solution)/shard_map/psum | solution.py:28
  242.4 0.9 divide_convert_fusion.2
  243.3 2.3 fusion.13
  245.6 0.7 all_gather_reshape.3
  246.3 0.0 all-gather.2.cloned.1.call-update
  246.3 47.1 %all-gather.2.cloned.1.call-done = f32[16,8,2048]{2,1,0:T(8,128)} async-done(((f32[1,8,2048]{2,1,0:T(8,128)}), f32[16,8,2048]{2,1,0:T(8,128)}) %all-gather.2.cloned.1.call-update) | async-done | bytes 1048592 | tf_op jit(solution)/shard_map/all_gather | solution.py:38
  293.4 1.3 reduce_sum.29
  294.7 21.1 %all_gather.7 = bf16[128,2048]{1,0:T(8,128)(2,1)S(1)} all-gather(bf16[8,2048]{1,0:T(8,128)(2,1)S(1)} %reduce_sum.29), channel_id=1, replica_groups=mesh['dp'=16,'expert'=16] {'expert'}, dimensions={0}, use_global_device_ids=true | all-gather | bytes 557056 | tf_op jit(solution)/shard_map/all_gather | solution.py:40
  315.9 3.3 %convolution_convert_fusion = bf16[1024,2048]{1,0:T(8,128)(2,1)} fusion(bf16[128,2048]{1,0:T(8,128)(2,1)S(1)} %all_gather.7, f32[1024,128]{1,0:T(8,128)S(1)} %get-tuple-element.10, f32[1024]{0:T(1024)S(1)} %get-tuple-element.5, f32[1024]{0:T(1024)S(1)} %get-tuple-element.9), kind=kOutput, calls=%fused_computation | convolution fusion | flops 539361280 | bytes 5251072 | tf_op jit(solution)/shard_map/dot_general | solution.py:41
  (6 shorter events, 0.0 us)
Async XLA Ops:
  6.5 236.8 %copy-start = (bf16[2,256,2048]{2,1,0:T(8,128)(2,1)S(1)}, bf16[2,256,2048]{2,1,0:T(8,128)(2,1)}, u32[]{:S(2)}) copy-start(bf16[2,256,2048]{2,1,0:T(8,128)(2,1)} %param.9) | copy-start | bytes 6291460
  6.5 141.0 %reduce-scatter.2.cloned.1.call-start = ((), (), s32[]{:S(2)}) async-start(), calls=%async_computation.1 | async-start | bytes 1114112 | tf_op jit(solution)/shard_map/reduce_scatter | solution.py:25
  11.0 136.6 %copy-start.1 = (u32[256]{0:T(256)S(1)}, u32[256]{0:T(256)}, u32[]{:S(2)}) copy-start(u32[256]{0:T(256)} %constant.22) | copy-start | bytes 3076
  96.9 145.5 %all-reduce.3.cloned.1.call-start = ((), (), s32[]{:S(2)}) async-start(), calls=%async_computation.2 | async-start | bytes 131072 | tf_op jit(solution)/shard_map/psum | solution.py:28
  147.5 145.9 %all-gather.2.cloned.1.call-start = ((), (), s32[]{:S(2)}) async-start(), calls=%async_computation.3 | async-start | bytes 1114112 | tf_op jit(solution)/shard_map/all_gather | solution.py:38
Sparse Core Ops, SparseCore 0:
  97.0 50.4 reduce-scatter.1
  150.7 91.6 all-reduce.2
  246.5 46.9 all-gather.1
